TPU v7x, 32 devices: a whole 2x2x4 slice. The times are simulated.
32 devices in a mesh: ctx: 8 (over z, y), head: 4 (over x, core).
Axes of the slice: x: 2, y: 2, z: 4, core: 2. Of those that a mesh axis runs over, the one named last changes fastest.
Arguments:
- query_all: bfloat16 [1024, 1024], P('ctx', 'head'), may hold values from -6 to 6
- key_all: bfloat16 [1024, 1024], P('ctx', 'head'), may hold values from -6 to 6
- value_all: bfloat16 [1024, 1024], P('ctx', 'head'), may hold values from -6 to 6
- cotangent: bfloat16 [1024, 1024], P('ctx', 'head'), may hold values from -6 to 6
- conv_input: bfloat16 [1024, 1024], P('ctx', 'head'), may hold values from -6 to 6
- rec_lengths: int32 [3], replicated, may hold values from 170 to 341
- out_proj: bfloat16 [1024, 1024], P(None, 'head'), may hold values from -0.1875 to 0.1875
- conv_weight: bfloat16 [31, 1024], P(None, 'head'), may hold values from -1 to 1
Outputs:
- q_grad: bfloat16 [1024, 1024], P('ctx', 'head')
- k_grad: bfloat16 [1024, 1024], P('ctx', 'head')
- v_grad: bfloat16 [1024, 1024], P('ctx', 'head')
- x_grad: bfloat16 [1024, 1024], P('ctx', 'head')
- out_proj_grad: float32 [1024, 1024], P('ctx', 'head')
- conv_weight_grad: float32 [31, 1024], P(None, 'head')
Inputs may be any that keep to these rules, and one draw needn't show every extreme that they name: `rec_lengths`: the recordings lie end to end from frame 0; frames from their total on are padding.
All inputs are finite; a program needn't handle non-finite values.
Results may differ from a plain program's by a relative error of at most 0.03.
Values may be sent and summed in bfloat16 or wider, within the bound.
No kernel may reach another device: no remote copies, remote signals or barrier semaphores. Data moves between devices by JAX's collectives and lax.ppermute only.
A program may use at most 64 MiB of HBM per device.

v0:
```python
import jax
import jax.numpy as jnp
from jax import lax
from jax.sharding import PartitionSpec as P

HEAD_DIM = 64


def extended_2(block, sides, width):
    for axis, dim in sides:
        count = lax.axis_size(axis)
        forward = [(i, i + 1) for i in range(count - 1)]
        backward = [(target, source) for source, target in forward]
        low = lax.ppermute(
            lax.slice_in_dim(block, block.shape[dim] - width, None, axis=dim), axis, forward
        )
        high = lax.ppermute(lax.slice_in_dim(block, 0, width, axis=dim), axis, backward)
        block = jnp.concatenate([low, block, high], axis=dim)
    return block


def split_heads(matrix):
    return matrix.reshape(matrix.shape[0], -1, HEAD_DIM)


def join_heads(tensor):
    return jnp.transpose(tensor, (1, 0, 2)).reshape(tensor.shape[1], -1)


def over_blocks(step_fn, running, members):
    row_count = members[0].shape[0]
    blocks = row_count // 512
    stacked = tuple((member.reshape((blocks, 512) + member.shape[1:]) for member in members))

    def inner_step(state, inputs):
        block_members, block_index = inputs
        return (step_fn(state, block_members, block_index * 512), None)

    running, unused = lax.scan(inner_step, running, (stacked, jnp.arange(blocks, dtype=jnp.int32)))
    return running


def conv_forward(extended, taps, frames):
    wide = extended.astype(jnp.float32)
    weights = taps.astype(jnp.float32)
    result = jnp.zeros((frames, extended.shape[1]), jnp.float32)
    for offset in range(taps.shape[0]):
        result = result + weights[offset] * wide[offset : offset + frames]
    return result


def conv_backward(grad_ext, taps, frames):
    wide = grad_ext.astype(jnp.float32)
    weights = taps.astype(jnp.float32)
    reach = taps.shape[0] - 1
    result = jnp.zeros((frames, grad_ext.shape[1]), jnp.float32)
    for offset in range(taps.shape[0]):
        result = result + weights[offset] * wide[reach - offset : reach - offset + frames]
    return result


def tap_products(grad_conv, extended):
    frames = grad_conv.shape[0]
    wide = extended.astype(jnp.float32)
    grad_wide = grad_conv.astype(jnp.float32)
    rows_out = [
        jnp.sum(grad_wide * wide[offset : offset + frames], axis=0)
        for offset in range(extended.shape[0] - frames + 1)
    ]
    return jnp.stack(rows_out)


def gate_slope(conv_out, upstream):
    sigmoid_value = jax.nn.sigmoid(conv_out)
    return (
        upstream.astype(jnp.float32) * sigmoid_value * (1.0 + conv_out * (1.0 - sigmoid_value))
    ).astype(jnp.bfloat16)


def on_device(
    query_all, key_all, value_all, cotangent, conv_input, rec_lengths, out_proj, conv_weight
):
    frames, local_width = query_all.shape
    half_taps = conv_weight.shape[0] // 2
    score_scale = HEAD_DIM ** (-0.5)
    valid_total = jnp.sum(rec_lengths)
    positions = lax.axis_index("ctx") * frames + jnp.arange(frames, dtype=jnp.int32)
    frame_ok = positions < valid_total
    masked = jnp.where(frame_ok[:, None], conv_input, jnp.zeros_like(conv_input))
    input_ext = extended_2(masked, (("ctx", 0),), half_taps)
    conv_out = conv_forward(input_ext, conv_weight, frames)
    grad_conv = gate_slope(conv_out, cotangent)
    grad_ext = extended_2(grad_conv, (("ctx", 0),), half_taps)
    conv_weight_grad = lax.psum(tap_products(grad_conv, input_ext), "ctx")
    grad_input = conv_backward(grad_ext, conv_weight, frames)
    x_grad = (cotangent.astype(jnp.float32) + jnp.where(frame_ok[:, None], grad_input, 0.0)).astype(
        jnp.bfloat16
    )
    full_grad = lax.all_gather(x_grad, "head", axis=1, tiled=True)
    grad_out16 = jnp.dot(full_grad, out_proj, preferred_element_type=jnp.float32).astype(
        jnp.bfloat16
    )
    query_heads = split_heads(query_all)
    grad_heads = split_heads(grad_out16)
    grad_wide = grad_heads.astype(jnp.float32)
    heads_here = query_heads.shape[1]
    start_max = jnp.full((heads_here, frames), -1e30, jnp.float32)
    zeros_sum = jnp.zeros((heads_here, frames), jnp.float32)
    zeros_acc = jnp.zeros((heads_here, frames, HEAD_DIM), jnp.float32)
    zeros_keys = jnp.zeros((frames, heads_here, HEAD_DIM), jnp.float32)

    def masked_scores(key_rows, first_row):
        scores = (
            jnp.einsum(
                "qhd,khd->hqk",
                query_heads,
                split_heads(key_rows),
                preferred_element_type=jnp.float32,
            )
            * score_scale
        )
        key_ok = first_row + jnp.arange(key_rows.shape[0], dtype=jnp.int32) < valid_total
        return jnp.where(key_ok[None, None, :], scores, -jnp.inf)

    def forward_step(running, members, first_row):
        maxima, totals, numer = running
        key_rows, value_rows = members
        scores = masked_scores(key_rows, first_row)
        new_max = jnp.maximum(maxima, jnp.max(scores, axis=-1))
        shrink = jnp.exp(maxima - new_max)
        weights = jnp.exp(scores - new_max[..., None])
        totals = totals * shrink + jnp.sum(weights, axis=-1)
        numer = numer * shrink[..., None] + jnp.einsum(
            "hqk,khd->hqd",
            weights.astype(jnp.bfloat16),
            split_heads(value_rows),
            preferred_element_type=jnp.float32,
        )
        return (new_max, totals, numer)

    maxima, totals, numer = over_blocks(
        forward_step,
        (start_max, zeros_sum, zeros_acc),
        (
            lax.all_gather(key_all, "ctx", axis=0, tiled=True),
            lax.all_gather(value_all, "ctx", axis=0, tiled=True),
        ),
    )
    attn_out = numer / totals[..., None]
    log_total = maxima + jnp.log(totals)
    row_delta = jnp.einsum("qhd,hqd->hq", grad_wide, attn_out)
    query_sum = None

    def query_step(running, members, first_row):
        key_rows, value_rows = members
        scores = masked_scores(key_rows, first_row)
        probs = jnp.exp(scores - log_total[..., None])
        slopes = jnp.einsum(
            "qhd,khd->hqk", grad_heads, split_heads(value_rows), preferred_element_type=jnp.float32
        )
        dscores = probs * (slopes - row_delta[..., None])
        return running + jnp.einsum(
            "hqk,khd->hqd",
            dscores,
            split_heads(key_rows).astype(jnp.float32),
            precision=lax.Precision.HIGHEST,
        )

    query_sum = over_blocks(
        query_step,
        zeros_acc,
        (
            lax.all_gather(key_all, "ctx", axis=0, tiled=True),
            lax.all_gather(value_all, "ctx", axis=0, tiled=True),
        ),
    )
    lse_all, delta_all = (
        lax.all_gather(log_total, "ctx", axis=1, tiled=True),
        lax.all_gather(row_delta, "ctx", axis=1, tiled=True),
    )
    key_heads = split_heads(key_all)
    value_heads = split_heads(value_all)

    def key_step(running, members, first_row):
        key_acc, value_acc = running
        query_rows, grad_rows = members
        rows_here = query_rows.shape[0]
        lse_rows = lax.dynamic_slice_in_dim(lse_all, first_row, rows_here, 1)
        delta_rows = lax.dynamic_slice_in_dim(delta_all, first_row, rows_here, 1)
        scores = (
            jnp.einsum(
                "qhd,khd->hqk",
                split_heads(query_rows),
                key_heads,
                preferred_element_type=jnp.float32,
            )
            * score_scale
        )
        scores = jnp.where(frame_ok[None, None, :], scores, -jnp.inf)
        probs = jnp.exp(scores - lse_rows[..., None])
        probs16 = probs.astype(jnp.bfloat16)
        slopes = jnp.einsum(
            "qhd,khd->hqk", split_heads(grad_rows), value_heads, preferred_element_type=jnp.float32
        )
        dscores16 = (probs * (slopes - delta_rows[..., None])).astype(jnp.bfloat16)
        key_acc = key_acc + jnp.einsum(
            "hqk,qhd->khd", dscores16, split_heads(query_rows), preferred_element_type=jnp.float32
        )
        value_acc = value_acc + jnp.einsum(
            "hqk,qhd->khd", probs16, split_heads(grad_rows), preferred_element_type=jnp.float32
        )
        return (key_acc, value_acc)

    key_sum, value_sum = over_blocks(
        key_step,
        (zeros_keys, zeros_keys),
        (
            lax.all_gather(query_all, "ctx", axis=0, tiled=True),
            lax.all_gather(grad_out16, "ctx", axis=0, tiled=True),
        ),
    )
    q_grad = join_heads(query_sum * score_scale).astype(jnp.bfloat16)
    attn16 = join_heads(attn_out).astype(jnp.bfloat16)
    k_grad = (key_sum * score_scale).reshape(frames, local_width).astype(jnp.bfloat16)
    v_grad = value_sum.reshape(frames, local_width).astype(jnp.bfloat16)
    out_proj_grad = lax.psum_scatter(
        jnp.einsum("ta,tb->ab", full_grad, attn16, preferred_element_type=jnp.float32),
        "ctx",
        scatter_dimension=0,
        tiled=True,
    )
    return (q_grad, k_grad, v_grad, x_grad, out_proj_grad, conv_weight_grad)


def solution(mesh):
    placed = (
        P("ctx", "head"),
        P("ctx", "head"),
        P("ctx", "head"),
        P("ctx", "head"),
        P("ctx", "head"),
        P(),
        P(None, "head"),
        P(None, "head"),
    )
    return jax.shard_map(
        on_device,
        mesh=mesh,
        in_specs=placed,
        out_specs=(
            P("ctx", "head"),
            P("ctx", "head"),
            P("ctx", "head"),
            P("ctx", "head"),
            P("ctx", "head"),
            P(None, "head"),
        ),
        check_vma=False,
    )
```

profile of v0, /device:TPU:0, one launch (start us, length us, event | category | flops | bytes accessed | tf_op | source)
XLA Modules:
  0.0 354.8 jit_solution(6739002948123425645)
XLA Ops:
  10.9 1.3 collective-permute-start.1
  12.2 6.1 %collective-permute-start = (bf16[15,256]{1,0:T(8,128)(2,1)}, bf16[15,256]{1,0:T(8,128)(2,1)}, u32[]{:S(2)}, u32[]{:S(2)}) collective-permute-start(bf16[15,256]{1,0:T(8,128)(2,1)} %get-tuple-element.482), channel_id=1, source_target_pairs={{0,4},{4,8},{8,12},{12,16},{16,20},{20,24},{24,28},{1,5},{5,9},{9,... | collective-permute-start | bytes 23048 | tf_op jit(solution)/shard_map/ppermute | solution.py:14
  20.4 32.4 %all_gather.26 = bf16[1024,256]{1,0:T(8,128)(2,1)S(1)} all-gather(bf16[128,256]{1,0:T(8,128)(2,1)S(1)} %copy-done.13), channel_id=1, replica_groups=mesh['ctx'=8,'head'=4] {'ctx'}, dimensions={0}, use_global_device_ids=true | all-gather | bytes 589824 | tf_op jit(solution)/shard_map/all_gather | solution.py:218
  52.8 31.2 %all_gather.23 = bf16[1024,256]{1,0:T(8,128)(2,1)S(1)} all-gather(bf16[128,256]{1,0:T(8,128)(2,1)S(1)} %copy-done.14), channel_id=1, replica_groups=mesh['ctx'=8,'head'=4] {'ctx'}, dimensions={0}, use_global_device_ids=true | all-gather | bytes 589824 | tf_op jit(solution)/shard_map/all_gather | solution.py:173
  84.8 31.2 %all_gather.24 = bf16[1024,256]{1,0:T(8,128)(2,1)S(1)} all-gather(bf16[128,256]{1,0:T(8,128)(2,1)S(1)} %copy-done.15), channel_id=1, replica_groups=mesh['ctx'=8,'head'=4] {'ctx'}, dimensions={0}, use_global_device_ids=true | all-gather | bytes 589824 | tf_op jit(solution)/shard_map/all_gather | solution.py:174
  116.2 9.9 %while.39 = (s32[]{:T(128)}, f32[4,128]{1,0:T(4,128)S(1)}, f32[4,128]{1,0:T(4,128)S(1)}, f32[4,128,64]{1,2,0:T(8,128)S(1)}, s32[2]{0:T(128)S(1)}, /*index=5*/s32...) while((s32[]{:T(128)}, f32[4,128]{1,0:T(4,128)S(1)}, ...), condition=%wide.region_4.5_spmd.clone, body=%wide.region_1.4_spmd.clone.sunk | while | flops 69045760 | bytes 5080357 | solution.py:39
  118.8 1.2 fusion.146
  123.7 1.2 fusion.146
  126.8 1.6 copy.44
  129.1 26.8 %all_gather.27 = f32[4,1024]{1,0:T(4,128)} all-gather(f32[4,128]{1,0:T(4,128)S(1)} %log_add_fusion), channel_id=1, replica_groups=mesh['ctx'=8,'head'=4] {'ctx'}, dimensions={1}, use_global_device_ids=true | all-gather | bytes 18432 | tf_op jit(solution)/shard_map/all_gather | solution.py:178
  159.0 1.3 collective-permute-start.3
  160.3 4.5 %collective-permute-start.2 = (bf16[15,256]{1,0:T(8,128)(2,1)S(1)}, bf16[15,256]{1,0:T(8,128)(2,1)S(1)}, u32[]{:S(2)}, u32[]{:S(2)}) collective-permute-start(bf16[15,256]{1,0:T(8,128)(2,1)S(1)} %get-tuple-element.480), channel_id=1, source_target_pairs={{0,4},{4,8},{8,12},{12,16},{16,20},{20,24},{24,28},{1,5},{5,9},{9,... | collective-permute-start | bytes 23048 | tf_op jit(solution)/shard_map/ppermute | solution.py:14
  164.9 34.5 %psum.7 = f32[31,256]{1,0:T(8,128)} all-reduce(f32[31,256]{1,0:T(8,128)S(1)} %stack.127), channel_id=1, replica_groups=mesh['ctx'=8,'head'=4] {'ctx'}, use_global_device_ids=true, to_apply=%region_41.42 | all-reduce | flops 7936 | bytes 63488 | tf_op jit(solution)/shard_map/psum | solution.py:94
  201.2 5.8 %all_gather.25 = bf16[128,1024]{1,0:T(8,128)(2,1)S(1)} all-gather(bf16[128,256]{1,0:T(8,128)(2,1)S(1)} %fusion.26), channel_id=1, replica_groups=mesh['ctx'=8,'head'=4] {'head'}, dimensions={1}, use_global_device_ids=true | all-gather | bytes 327680 | tf_op jit(solution)/shard_map/all_gather | solution.py:99
  208.6 33.5 %all_gather.28 = bf16[1024,256]{1,0:T(8,128)(2,1)} all-gather(bf16[128,256]{1,0:T(8,128)(2,1)S(1)} %convolution_convert_fusion), channel_id=1, replica_groups=mesh['ctx'=8,'head'=4] {'ctx'}, dimensions={0}, use_global_device_ids=true | all-gather | bytes 589824 | tf_op jit(solution)/shard_map/all_gather | solution.py:219
  242.2 1.5 fusion.90
  243.6 27.0 %all_gather.29 = f32[4,1024]{1,0:T(4,128)} all-gather(f32[4,128]{1,0:T(4,128)S(1)} %get-tuple-element.773), channel_id=1, replica_groups=mesh['ctx'=8,'head'=4] {'ctx'}, dimensions={1}, use_global_device_ids=true | all-gather | bytes 18432 | tf_op jit(solution)/shard_map/all_gather | solution.py:179
  270.6 12.2 %while.40 = (s32[]{:T(128)}, f32[4,128,64]{1,2,0:T(8,128)}, s32[2]{0:T(128)S(1)}, s32[]{:T(128)}, bf16[2,512,256]{1,2,0:T(8,128)(2,1)S(1)}, /*index=5*/bf16[128,...) while((s32[]{:T(128)}, f32[4,128,64]{1,2,0:T(8,128)}, ...), condition=%wide.region_6.7_spmd.clone, body=%wide.region_5.6_spmd.clone.sunk | while | flops 269812736 | bytes 6427827 | solution.py:39
  272.6 1.3 fusion.155
  273.9 1.2 fusion.156
  275.1 1.2 convolution_add_fusion.5
  278.2 1.3 fusion.155
  279.5 1.2 fusion.156
  280.7 2.1 convolution_add_fusion.5
  284.6 1.3 fusion.97
  286.0 1.0 copy-done.1
  287.0 13.6 %while.41 = (s32[]{:T(128)}, f32[128,4,64]{0,2,1:T(8,128)S(1)}, f32[128,4,64]{0,2,1:T(8,128)}, bf16[2,512,256]{2,1,0:T(8,128)(2,1)S(1)}, bf16[128,4,64]{0,2,1:T(...) while((s32[]{:T(128)}, f32[128,4,64]{0,2,1:T(8,128)S(1)}, ...), condition=%wide.region_8.9_spmd.clone, body=%wide.region_7.8_spmd.clone.sunk | while | flops 136184064 | bytes 8045098 | solution.py:39
  289.8 1.3 fusion.164
  291.3 1.5 fusion.165
  296.6 1.3 fusion.164
  298.1 1.6 fusion.165
  302.3 45.7 %reduce-scatter.2.cloned.1.call-done = f32[128,256]{1,0:T(8,128)} async-done(((f32[1024,256]{1,0:T(8,128)}), f32[128,256]{1,0:T(8,128)}) %reduce-scatter.2.cloned.1.call-update) | async-done | bytes 131088 | tf_op jit(solution)/shard_map/reduce_scatter | solution.py:226
  (192 shorter events, 32.7 us)
Async XLA Ops:
  7.2 200.5 %copy-start = (bf16[1024,256]{1,0:T(8,128)(2,1)S(1)}, bf16[1024,256]{1,0:T(8,128)(2,1)}, u32[]{:S(2)}) copy-start(bf16[1024,256]{1,0:T(8,128)(2,1)} %param.20) | copy-start | bytes 1572868
  7.2 340.7 %reduce-scatter.2.cloned.1.call-start = ((), (), s32[]{:S(2)}) async-start(), calls=%async_computation.1 | async-start | bytes 1179648 | tf_op jit(solution)/shard_map/reduce_scatter | solution.py:226
  9.4 9.0 %copy-start.18 = (bf16[31,256]{1,0:T(8,128)(2,1)S(1)}, bf16[31,256]{1,0:T(8,128)(2,1)}, u32[]{:S(2)}) copy-start(bf16[31,256]{1,0:T(8,128)(2,1)} %param.21) | copy-start | bytes 47620
  10.3 9.3 %copy-start.9 = (bf16[128,256]{1,0:T(8,128)(2,1)}, bf16[128,256]{1,0:T(8,128)(2,1)S(1)}, u32[]{:S(2)}) copy-start(bf16[128,256]{1,0:T(8,128)(2,1)S(1)} %broadcast_select_fusion) | copy-start | bytes 196612
  10.3 9.3 %copy-start.13 = (bf16[128,256]{1,0:T(8,128)(2,1)S(1)}, bf16[128,256]{1,0:T(8,128)(2,1)}, u32[]{:S(2)}) copy-start(bf16[128,256]{1,0:T(8,128)(2,1)} %param.14) | copy-start | bytes 196612
  10.9 145.0 %collective-permute-start.1 = (bf16[15,256]{1,0:T(8,128)(2,1)}, bf16[15,256]{1,0:T(8,128)(2,1)}, u32[]{:S(2)}, u32[]{:S(2)}) collective-permute-start(bf16[15,256]{1,0:T(8,128)(2,1)} %get-tuple-element.483), channel_id=1, source_target_pairs={{4,0},{8,4},{12,8},{16,12},{20,16},{24,20},{28,24},{5,1},{9,5},{13... | collective-permute-start | bytes 23048 | tf_op jit(solution)/shard_map/ppermute | solution.py:17
  12.2 143.7 %collective-permute-start = (bf16[15,256]{1,0:T(8,128)(2,1)}, bf16[15,256]{1,0:T(8,128)(2,1)}, u32[]{:S(2)}, u32[]{:S(2)}) collective-permute-start(bf16[15,256]{1,0:T(8,128)(2,1)} %get-tuple-element.482), channel_id=1, source_target_pairs={{0,4},{4,8},{8,12},{12,16},{16,20},{20,24},{24,28},{1,5},{5,9},{9,... | collective-permute-start | bytes 23048 | tf_op jit(solution)/shard_map/ppermute | solution.py:14
  20.4 32.4 %copy-start.14 = (bf16[128,256]{1,0:T(8,128)(2,1)S(1)}, bf16[128,256]{1,0:T(8,128)(2,1)}, u32[]{:S(2)}) copy-start(bf16[128,256]{1,0:T(8,128)(2,1)} %param.15) | copy-start | bytes 196612
  126.8 1.6 copy-start.16
  128.4 27.6 %copy-start.10 = (bf16[128,256]{1,0:T(8,128)(2,1)S(1)}, bf16[128,256]{1,0:T(8,128)(2,1)}, u32[]{:S(2)}) copy-start(bf16[128,256]{1,0:T(8,128)(2,1)} %copy-done.9) | copy-start | bytes 196612
  156.0 1.1 copy-start.20
  156.0 1.1 copy-start.21
  156.0 1.1 copy-start.22
  156.0 1.1 copy-start.23
  156.0 1.1 copy-start.24
  156.0 1.1 copy-start.25
  156.0 1.1 copy-start.26
  156.0 1.1 copy-start.27
  156.1 1.1 copy-start.28
  156.1 1.1 copy-start.29
  156.1 1.1 copy-start.30
  156.1 1.1 copy-start.31
  156.1 1.1 copy-start.32
  156.1 1.1 copy-start.33
  156.1 1.1 copy-start.34
  156.1 1.1 copy-start.35
  159.0 40.5 %collective-permute-start.3 = (bf16[15,256]{1,0:T(8,128)(2,1)S(1)}, bf16[15,256]{1,0:T(8,128)(2,1)S(1)}, u32[]{:S(2)}, u32[]{:S(2)}) collective-permute-start(bf16[15,256]{1,0:T(8,128)(2,1)S(1)} %get-tuple-element.481), channel_id=1, source_target_pairs={{4,0},{8,4},{12,8},{16,12},{20,16},{24,20},{28,24},{5,1},{9,5},{13... | collective-permute-start | bytes 23048 | tf_op jit(solution)/shard_map/ppermute | solution.py:17
  160.3 39.2 %collective-permute-start.2 = (bf16[15,256]{1,0:T(8,128)(2,1)S(1)}, bf16[15,256]{1,0:T(8,128)(2,1)S(1)}, u32[]{:S(2)}, u32[]{:S(2)}) collective-permute-start(bf16[15,256]{1,0:T(8,128)(2,1)S(1)} %get-tuple-element.480), channel_id=1, source_target_pairs={{0,4},{4,8},{8,12},{12,16},{16,20},{20,24},{24,28},{1,5},{5,9},{9,... | collective-permute-start | bytes 23048 | tf_op jit(solution)/shard_map/ppermute | solution.py:14
  208.6 33.5 %copy-start.6 = (f32[4,128,64]{1,2,0:T(8,128)S(1)}, f32[4,128,64]{1,2,0:T(8,128)}, u32[]{:S(2)}) copy-start(f32[4,128,64]{1,2,0:T(8,128)} %copy-done.5) | copy-start | bytes 393220
  282.8 1.7 copy-start.8
  291.3 1.6 copy-start.2
  298.1 1.6 copy-start.2
  (31 other events, 27.1 us)
Sparse Core Ops, SparseCore 0:
  286.1 61.7 reduce-scatter.1
where the time goes:
time: 356 us; the launch traced here: 355 us
  blocking collectives  222 us (62%)
  waiting for transfers between devices  45.7 us (13%)
  local copies, waits for them, and re-layouts  23.8 us (7%)
  matrix products  19.1 us (5%)
  between operations  14.7 us (4%)
  starting transfers between devices  13.3 us (4%)
  other arithmetic  11.6 us (3%)
  loops' own time  4.23 us (1%)
    reduce_scatter x1, waiting for transfers between devices, on_device(): lax.psum_scatter(jnp.einsum('ta,tb->ab', full_grad, attn16, preferred_ele...  45.7 us
    psum x1, blocking collectives, on_device(): conv_weight_grad = lax.psum(tap_products(grad_conv, input_ext), 'ctx')  34.5 us
    all_gather x1, blocking collectives, on_device(): lax.all_gather(grad_out16, 'ctx', axis=0, tiled=True)  33.5 us
    all_gather x1, blocking collectives, on_device(): lax.all_gather(query_all, 'ctx', axis=0, tiled=True)  32.4 us
    all_gather x1, blocking collectives, on_device(): lax.all_gather(value_all, 'ctx', axis=0, tiled=True)  31.2 us
    all_gather x1, blocking collectives, on_device(): lax.all_gather(key_all, 'ctx', axis=0, tiled=True)  31.2 us
    all_gather x1, blocking collectives, on_device(): lax.all_gather(row_delta, 'ctx', axis=1, tiled=True)  27 us
    all_gather x1, blocking collectives, on_device(): lax.all_gather(log_total, 'ctx', axis=1, tiled=True)  26.8 us
  transfers between devices with their start and end apart: 5, of which 1 were waited for; matrix products, arithmetic and copies ran while one was open for 7% of the time, Pallas kernels for 0%

commit v1 on v0

--- a/solution.py
+++ b/solution.py
@@ -91,7 +91,9 @@
     conv_out = conv_forward(input_ext, conv_weight, frames)
     grad_conv = gate_slope(conv_out, cotangent)
     grad_ext = extended_2(grad_conv, (("ctx", 0),), half_taps)
-    conv_weight_grad = lax.psum(tap_products(grad_conv, input_ext), "ctx")
+    own = tap_products(grad_conv, input_ext)
+    parts = lax.all_gather(own, "ctx", axis=0, tiled=False)
+    conv_weight_grad = parts.sum(axis=0)
     grad_input = conv_backward(grad_ext, conv_weight, frames)
     x_grad = (cotangent.astype(jnp.float32) + jnp.where(frame_ok[:, None], grad_input, 0.0)).astype(
         jnp.bfloat16

time: 356 us -> 353 us (level)
    psum x1 -> x0, blocking collectives: 34.5 us -> none  [on_device(): conv_weight_grad = lax.psum(tap_products(grad_conv, input_ext), 'ctx')]
    all_gather x0 -> x1, blocking collectives: none -> 30.9 us  [on_device(): parts = lax.all_gather(own, 'ctx', axis=0, tiled=False)]
where the time goes in v1:
time: 353 us; the launch traced here: 352 us
  blocking collectives  219 us (62%)
  waiting for transfers between devices  45.6 us (13%)
  local copies, waits for them, and re-layouts  23.8 us (7%)
  matrix products  19.1 us (5%)
  between operations  14.7 us (4%)
  starting transfers between devices  13.3 us (4%)
  other arithmetic  12.3 us (3%)
  loops' own time  4.23 us (1%)
    reduce_scatter x1, waiting for transfers between devices, on_device(): lax.psum_scatter(jnp.einsum('ta,tb->ab', full_grad, attn16, preferred_ele...  45.6 us
    all_gather x1, blocking collectives, on_device(): lax.all_gather(grad_out16, 'ctx', axis=0, tiled=True)  33.5 us
    all_gather x1, blocking collectives, on_device(): lax.all_gather(query_all, 'ctx', axis=0, tiled=True)  32.4 us
    all_gather x1, blocking collectives, on_device(): lax.all_gather(value_all, 'ctx', axis=0, tiled=True)  31.2 us
    all_gather x1, blocking collectives, on_device(): lax.all_gather(key_all, 'ctx', axis=0, tiled=True)  31.2 us
    all_gather x1, blocking collectives, on_device(): parts = lax.all_gather(own, 'ctx', axis=0, tiled=False)  30.9 us
    all_gather x1, blocking collectives, on_device(): lax.all_gather(row_delta, 'ctx', axis=1, tiled=True)  27 us
    all_gather x1, blocking collectives, on_device(): lax.all_gather(log_total, 'ctx', axis=1, tiled=True)  26.8 us
  transfers between devices with their start and end apart: 5, of which 1 were waited for; matrix products, arithmetic and copies ran while one was open for 7% of the time, Pallas kernels for 0%

profile of v1, /device:TPU:0, one launch (start us, length us, event | category | flops | bytes accessed | tf_op | source)
XLA Modules:
  0.0 351.7 jit_solution(7023921871371628992)
XLA Ops:
  10.9 1.3 collective-permute-start.1
  12.2 6.1 %collective-permute-start = (bf16[15,256]{1,0:T(8,128)(2,1)}, bf16[15,256]{1,0:T(8,128)(2,1)}, u32[]{:S(2)}, u32[]{:S(2)}) collective-permute-start(bf16[15,256]{1,0:T(8,128)(2,1)} %get-tuple-element.519), channel_id=1, source_target_pairs={{0,4},{4,8},{8,12},{12,16},{16,20},{20,24},{24,28},{1,5},{5,9},{9,... | collective-permute-start | bytes 23048 | tf_op jit(solution)/shard_map/ppermute | solution.py:14
  20.4 32.4 %all_gather.32 = bf16[1024,256]{1,0:T(8,128)(2,1)S(1)} all-gather(bf16[128,256]{1,0:T(8,128)(2,1)S(1)} %copy-done.13), channel_id=1, replica_groups=mesh['ctx'=8,'head'=4] {'ctx'}, dimensions={0}, use_global_device_ids=true | all-gather | bytes 589824 | tf_op jit(solution)/shard_map/all_gather | solution.py:220
  52.8 31.2 %all_gather.29 = bf16[1024,256]{1,0:T(8,128)(2,1)S(1)} all-gather(bf16[128,256]{1,0:T(8,128)(2,1)S(1)} %copy-done.14), channel_id=1, replica_groups=mesh['ctx'=8,'head'=4] {'ctx'}, dimensions={0}, use_global_device_ids=true | all-gather | bytes 589824 | tf_op jit(solution)/shard_map/all_gather | solution.py:175
  84.8 31.2 %all_gather.30 = bf16[1024,256]{1,0:T(8,128)(2,1)S(1)} all-gather(bf16[128,256]{1,0:T(8,128)(2,1)S(1)} %copy-done.15), channel_id=1, replica_groups=mesh['ctx'=8,'head'=4] {'ctx'}, dimensions={0}, use_global_device_ids=true | all-gather | bytes 589824 | tf_op jit(solution)/shard_map/all_gather | solution.py:176
  116.2 9.9 %while.39 = (s32[]{:T(128)}, f32[4,128]{1,0:T(4,128)S(1)}, f32[4,128]{1,0:T(4,128)S(1)}, f32[4,128,64]{1,2,0:T(8,128)S(1)}, s32[2]{0:T(128)S(1)}, /*index=5*/s32...) while((s32[]{:T(128)}, f32[4,128]{1,0:T(4,128)S(1)}, ...), condition=%wide.region_4.5_spmd.clone, body=%wide.region_1.4_spmd.clone.sunk | while | flops 69045760 | bytes 5080357 | solution.py:39
  118.8 1.2 fusion.146
  123.7 1.2 fusion.146
  126.8 1.6 copy.58
  129.1 26.8 %all_gather.33 = f32[4,1024]{1,0:T(4,128)} all-gather(f32[4,128]{1,0:T(4,128)S(1)} %log_add_fusion), channel_id=1, replica_groups=mesh['ctx'=8,'head'=4] {'ctx'}, dimensions={1}, use_global_device_ids=true | all-gather | bytes 18432 | tf_op jit(solution)/shard_map/all_gather | solution.py:180
  159.0 1.3 collective-permute-start.3
  160.3 4.5 %collective-permute-start.2 = (bf16[15,256]{1,0:T(8,128)(2,1)S(1)}, bf16[15,256]{1,0:T(8,128)(2,1)S(1)}, u32[]{:S(2)}, u32[]{:S(2)}) collective-permute-start(bf16[15,256]{1,0:T(8,128)(2,1)S(1)} %get-tuple-element.517), channel_id=1, source_target_pairs={{0,4},{4,8},{8,12},{12,16},{16,20},{20,24},{24,28},{1,5},{5,9},{9,... | collective-permute-start | bytes 23048 | tf_op jit(solution)/shard_map/ppermute | solution.py:14
  164.9 30.9 %all-gather.1 = f32[8,31,256]{2,1,0:T(8,128)S(1)} all-gather(f32[1,31,256]{2,1,0:T(8,128)S(1)} %bitcast.192), channel_id=2, replica_groups=mesh['ctx'=8,'head'=4] {'ctx'}, dimensions={0}, use_global_device_ids=true | all-gather | bytes 285696 | tf_op jit(solution)/shard_map/all_gather | solution.py:95
  198.2 5.8 %all_gather.31 = bf16[128,1024]{1,0:T(8,128)(2,1)S(1)} all-gather(bf16[128,256]{1,0:T(8,128)(2,1)S(1)} %fusion.26), channel_id=1, replica_groups=mesh['ctx'=8,'head'=4] {'head'}, dimensions={1}, use_global_device_ids=true | all-gather | bytes 327680 | tf_op jit(solution)/shard_map/all_gather | solution.py:101
  205.6 33.5 %all_gather.34 = bf16[1024,256]{1,0:T(8,128)(2,1)} all-gather(bf16[128,256]{1,0:T(8,128)(2,1)S(1)} %convolution_convert_fusion), channel_id=1, replica_groups=mesh['ctx'=8,'head'=4] {'ctx'}, dimensions={0}, use_global_device_ids=true | all-gather | bytes 589824 | tf_op jit(solution)/shard_map/all_gather | solution.py:221
  239.1 1.5 fusion.90
  240.6 27.0 %all_gather.35 = f32[4,1024]{1,0:T(4,128)} all-gather(f32[4,128]{1,0:T(4,128)S(1)} %get-tuple-element.810), channel_id=1, replica_groups=mesh['ctx'=8,'head'=4] {'ctx'}, dimensions={1}, use_global_device_ids=true | all-gather | bytes 18432 | tf_op jit(solution)/shard_map/all_gather | solution.py:181
  267.6 12.2 %while.40 = (s32[]{:T(128)}, f32[4,128,64]{1,2,0:T(8,128)}, s32[2]{0:T(128)S(1)}, s32[]{:T(128)}, bf16[2,512,256]{1,2,0:T(8,128)(2,1)S(1)}, /*index=5*/bf16[128,...) while((s32[]{:T(128)}, f32[4,128,64]{1,2,0:T(8,128)}, ...), condition=%wide.region_6.7_spmd.clone, body=%wide.region_5.6_spmd.clone.sunk | while | flops 269812736 | bytes 6427827 | solution.py:39
  269.5 1.3 fusion.155
  270.8 1.2 fusion.156
  272.0 1.2 convolution_add_fusion.5
  275.2 1.3 fusion.155
  276.4 1.2 fusion.156
  277.6 2.1 convolution_add_fusion.5
  281.5 1.3 fusion.97
  282.9 1.0 copy-done.1
  283.9 13.6 %while.41 = (s32[]{:T(128)}, f32[128,4,64]{0,2,1:T(8,128)S(1)}, f32[128,4,64]{0,2,1:T(8,128)}, bf16[2,512,256]{2,1,0:T(8,128)(2,1)S(1)}, bf16[128,4,64]{0,2,1:T(...) while((s32[]{:T(128)}, f32[128,4,64]{0,2,1:T(8,128)S(1)}, ...), condition=%wide.region_8.9_spmd.clone, body=%wide.region_7.8_spmd.clone.sunk | while | flops 136184064 | bytes 8045098 | solution.py:39
  286.7 1.3 fusion.164
  288.3 1.6 fusion.165
  293.6 1.3 fusion.164
  295.1 1.6 fusion.165
  299.2 45.6 %reduce-scatter.2.cloned.1.call-done = f32[128,256]{1,0:T(8,128)} async-done(((f32[1024,256]{1,0:T(8,128)}), f32[128,256]{1,0:T(8,128)}) %reduce-scatter.2.cloned.1.call-update) | async-done | bytes 131088 | tf_op jit(solution)/shard_map/reduce_scatter | solution.py:228
  (193 shorter events, 33.3 us)
Async XLA Ops:
  7.2 197.5 %copy-start = (bf16[1024,256]{1,0:T(8,128)(2,1)S(1)}, bf16[1024,256]{1,0:T(8,128)(2,1)}, u32[]{:S(2)}) copy-start(bf16[1024,256]{1,0:T(8,128)(2,1)} %param.20) | copy-start | bytes 1572868
  7.2 337.6 %reduce-scatter.2.cloned.1.call-start = ((), (), s32[]{:S(2)}) async-start(), calls=%async_computation.1 | async-start | bytes 1179648 | tf_op jit(solution)/shard_map/reduce_scatter | solution.py:228
  9.4 9.0 %copy-start.18 = (bf16[31,256]{1,0:T(8,128)(2,1)S(1)}, bf16[31,256]{1,0:T(8,128)(2,1)}, u32[]{:S(2)}) copy-start(bf16[31,256]{1,0:T(8,128)(2,1)} %param.21) | copy-start | bytes 47620
  10.3 9.3 %copy-start.9 = (bf16[128,256]{1,0:T(8,128)(2,1)}, bf16[128,256]{1,0:T(8,128)(2,1)S(1)}, u32[]{:S(2)}) copy-start(bf16[128,256]{1,0:T(8,128)(2,1)S(1)} %broadcast_select_fusion) | copy-start | bytes 196612
  10.3 9.3 %copy-start.13 = (bf16[128,256]{1,0:T(8,128)(2,1)S(1)}, bf16[128,256]{1,0:T(8,128)(2,1)}, u32[]{:S(2)}) copy-start(bf16[128,256]{1,0:T(8,128)(2,1)} %param.14) | copy-start | bytes 196612
  10.9 145.0 %collective-permute-start.1 = (bf16[15,256]{1,0:T(8,128)(2,1)}, bf16[15,256]{1,0:T(8,128)(2,1)}, u32[]{:S(2)}, u32[]{:S(2)}) collective-permute-start(bf16[15,256]{1,0:T(8,128)(2,1)} %get-tuple-element.520), channel_id=1, source_target_pairs={{4,0},{8,4},{12,8},{16,12},{20,16},{24,20},{28,24},{5,1},{9,5},{13... | collective-permute-start | bytes 23048 | tf_op jit(solution)/shard_map/ppermute | solution.py:17
  12.2 143.7 %collective-permute-start = (bf16[15,256]{1,0:T(8,128)(2,1)}, bf16[15,256]{1,0:T(8,128)(2,1)}, u32[]{:S(2)}, u32[]{:S(2)}) collective-permute-start(bf16[15,256]{1,0:T(8,128)(2,1)} %get-tuple-element.519), channel_id=1, source_target_pairs={{0,4},{4,8},{8,12},{12,16},{16,20},{20,24},{24,28},{1,5},{5,9},{9,... | collective-permute-start | bytes 23048 | tf_op jit(solution)/shard_map/ppermute | solution.py:14
  20.4 32.4 %copy-start.14 = (bf16[128,256]{1,0:T(8,128)(2,1)S(1)}, bf16[128,256]{1,0:T(8,128)(2,1)}, u32[]{:S(2)}) copy-start(bf16[128,256]{1,0:T(8,128)(2,1)} %param.15) | copy-start | bytes 196612
  126.8 1.6 copy-start.16
  128.4 27.6 %copy-start.10 = (bf16[128,256]{1,0:T(8,128)(2,1)S(1)}, bf16[128,256]{1,0:T(8,128)(2,1)}, u32[]{:S(2)}) copy-start(bf16[128,256]{1,0:T(8,128)(2,1)} %copy-done.9) | copy-start | bytes 196612
  156.0 1.1 copy-start.20
  156.0 1.1 copy-start.21
  156.0 1.1 copy-start.22
  156.0 1.1 copy-start.23
  156.0 1.1 copy-start.24
  156.0 1.1 copy-start.25
  156.0 1.1 copy-start.26
  156.0 1.1 copy-start.27
  156.0 1.1 copy-start.28
  156.1 1.1 copy-start.29
  156.1 1.1 copy-start.30
  156.1 1.1 copy-start.31
  156.1 1.1 copy-start.32
  156.1 1.1 copy-start.33
  156.1 1.1 copy-start.34
  156.1 1.1 copy-start.35
  159.0 37.5 %collective-permute-start.3 = (bf16[15,256]{1,0:T(8,128)(2,1)S(1)}, bf16[15,256]{1,0:T(8,128)(2,1)S(1)}, u32[]{:S(2)}, u32[]{:S(2)}) collective-permute-start(bf16[15,256]{1,0:T(8,128)(2,1)S(1)} %get-tuple-element.518), channel_id=1, source_target_pairs={{4,0},{8,4},{12,8},{16,12},{20,16},{24,20},{28,24},{5,1},{9,5},{13... | collective-permute-start | bytes 23048 | tf_op jit(solution)/shard_map/ppermute | solution.py:17
  160.3 36.2 %collective-permute-start.2 = (bf16[15,256]{1,0:T(8,128)(2,1)S(1)}, bf16[15,256]{1,0:T(8,128)(2,1)S(1)}, u32[]{:S(2)}, u32[]{:S(2)}) collective-permute-start(bf16[15,256]{1,0:T(8,128)(2,1)S(1)} %get-tuple-element.517), channel_id=1, source_target_pairs={{0,4},{4,8},{8,12},{12,16},{16,20},{20,24},{24,28},{1,5},{5,9},{9,... | collective-permute-start | bytes 23048 | tf_op jit(solution)/shard_map/ppermute | solution.py:14
  205.6 33.5 %copy-start.6 = (f32[4,128,64]{1,2,0:T(8,128)S(1)}, f32[4,128,64]{1,2,0:T(8,128)}, u32[]{:S(2)}) copy-start(f32[4,128,64]{1,2,0:T(8,128)} %copy-done.5) | copy-start | bytes 393220
  279.7 1.7 copy-start.8
  288.3 1.6 copy-start.2
  295.1 1.6 copy-start.2
  (31 other events, 27.1 us)
Sparse Core Ops, SparseCore 0:
  283.0 61.7 reduce-scatter.1
